TPU v7x, 32 devices: a whole 2x2x4 slice. The times are simulated.
32 devices in a mesh: groups: 2 (over y), seq: 4 (over z), mp: 2 (over x), section: 2 (over core).
Axes of the slice: x: 2, y: 2, z: 4, core: 2. Of those that a mesh axis runs over, the one named last changes fastest.
Arguments:
- features: bfloat16 [4, 512, 8192], P(('groups', 'section'), 'mp', 'seq'), parts along dimension 0, may hold values from -6 to 6
- alpha: float32 [512], P('mp'), may hold values from 0.5 to 2
- conv_weight: bfloat16 [1024, 32, 16], P('mp'), may hold values from -0.25 to 0.25
- qkv_weight: bfloat16 [1024, 3, 1024], P(None, None, 'mp'), may hold values from -1 to 1
- readout: float32 [1024], P('mp'), may hold values from -4 to 4
- offsets: int32 [4], P(('groups', 'section')), parts along dimension 0, may hold values from 0 to 14479
- pairs: int32 [8, 2], P('groups'), parts along dimension 0, may hold values from 0 to 1
- labels: int32 [8], P('groups'), parts along dimension 0, may hold values from 0 to 1
Outputs:
- grads: bfloat16 [3, 4, 1024, 1024], P(None, ('groups', 'section'), 'seq', 'mp'), parts along dimension 1
- rewards: float32 [4], P('groups'), parts along dimension 0
- loss: float32 [2], P('groups'), parts along dimension 0
There are 2 independent parts, one for each index of `groups`. A program takes and returns all parts, laid end to end along the dimension named above; an argument that names none is the same for every part. Nothing has to cross between parts.
All inputs are finite; a program needn't handle non-finite values.
Results may differ from a plain program's by a relative error of at most 0.017.
Values may be sent and summed in bfloat16 or wider, within the bound.
A program may use at most 64 MiB of HBM per device.

v0:
```python
import math
import jax
import jax.numpy as jnp
from jax import lax
from jax.sharding import PartitionSpec as P

D = 1024
HD = 64
EPS = 1e-06
BASE = 10000.0


def padded_2(block, sides, width):
    for axis, dim in sides:
        count = lax.axis_size(axis)
        forward = [(i, i + 1) for i in range(count - 1)]
        backward = [(target, source) for source, target in forward]
        low = lax.ppermute(
            lax.slice_in_dim(block, block.shape[dim] - width, None, axis=dim), axis, forward
        )
        high = lax.ppermute(lax.slice_in_dim(block, 0, width, axis=dim), axis, backward)
        block = jnp.concatenate([low, block, high], axis=dim)
    return block


def position_table(positions, feature_ids, width):
    pair_ids = (feature_ids // 2).astype(jnp.float32)
    freqs = jnp.exp(pair_ids * (-2.0 * math.log(BASE) / width))
    angle = positions.astype(jnp.float32)[..., None] * freqs
    return jnp.where(feature_ids % 2 == 0, jnp.sin(angle), jnp.cos(angle))


def local(features, alpha, conv_weight, qkv_weight, readout, offsets, pairs, labels):
    f32 = jnp.float32
    bf16 = jnp.bfloat16
    cand, chans, samples = features.shape
    local_width = conv_weight.shape[0]
    per_group = conv_weight.shape[1]
    kern = conv_weight.shape[2]
    stride = kern // 2
    frames_dev = samples // stride
    groups_here = chans // per_group
    heads_here = local_width // HD
    raw = features.astype(f32)
    slope = alpha[None, :, None]
    act = (raw + jnp.sin(slope * raw) ** 2 / slope).astype(bf16)
    padded = padded_2(act, (("seq", 2),), stride // 2)
    blocks = padded.reshape(cand, groups_here, per_group, frames_dev + 1, stride).transpose(
        0, 1, 3, 2, 4
    )
    patches = jnp.concatenate([blocks[:, :, :-1], blocks[:, :, 1:]], axis=-1).reshape(
        cand, groups_here, frames_dev, per_group * kern
    )
    kernel = conv_weight.reshape(groups_here, local_width // groups_here, per_group * kern)
    frames = jnp.einsum("cgfk,gok->cfgo", patches, kernel, preferred_element_type=f32).reshape(
        cand, frames_dev, local_width
    )
    slice_id = lax.axis_index("seq")
    part_id = lax.axis_index("mp")
    positions = (
        offsets[:, None] + slice_id * frames_dev + jnp.arange(frames_dev, dtype=jnp.int32)[None, :]
    )
    feature_ids = part_id * local_width + jnp.arange(local_width, dtype=jnp.int32)
    resid = (frames + position_table(positions, feature_ids, D)).astype(bf16)
    whole = lax.all_gather(resid, "mp", axis=2, tiled=True)
    squares = jnp.mean(jnp.square(whole.astype(f32)), axis=-1)
    projected = jnp.einsum("cfd,dtk->cftk", whole, qkv_weight, preferred_element_type=f32)
    qkv = (projected * lax.rsqrt(squares + EPS)[:, :, None, None]).astype(bf16)
    query = qkv[:, :, 0]
    keys, values = (
        lax.all_gather(qkv[:, :, 1], "seq", axis=1, tiled=True),
        lax.all_gather(qkv[:, :, 2], "seq", axis=1, tiled=True),
    )
    total = keys.shape[1]
    block = min(512, total)
    count_blocks = total // block
    scale = 1.0 / math.sqrt(HD)
    query4 = query.reshape(cand, frames_dev, heads_here, HD)

    def key_slice(source, start, size):
        return lax.dynamic_slice_in_dim(source, start, size, 1).reshape(cand, size, heads_here, HD)

    def scores_for(start, size):
        return (
            jnp.einsum(
                "cfhe,ckhe->chfk", query4, key_slice(keys, start, size), preferred_element_type=f32
            )
            * scale
        )

    def stat_step(carry, index):
        peak_now, mass_now = carry
        score = scores_for(index * block, block)
        fresh = jnp.maximum(peak_now, jnp.max(score, axis=-1))
        mass_now = mass_now * jnp.exp(peak_now - fresh) + jnp.sum(
            jnp.exp(score - fresh[..., None]), axis=-1
        )
        return ((fresh, mass_now), None)

    start_peak = jnp.full((cand, heads_here, frames_dev), -jnp.inf, f32)
    (peak, mass), _ = lax.scan(
        stat_step, (start_peak, jnp.zeros_like(start_peak)), jnp.arange(count_blocks)
    )

    def weights_for(start, size):
        return jnp.exp(scores_for(start, size) - peak[..., None]) / mass[..., None]

    def out_step(running, index):
        start = index * block
        prob = weights_for(start, block).astype(bf16)
        running = running + jnp.einsum(
            "chfk,ckhe->cfhe", prob, key_slice(values, start, block), preferred_element_type=f32
        )
        return (running, None)

    attended4, _ = lax.scan(
        out_step, jnp.zeros((cand, frames_dev, heads_here, HD), f32), jnp.arange(count_blocks)
    )
    attended = attended4.reshape(cand, frames_dev, local_width)
    gate = jax.nn.sigmoid(lax.optimization_barrier(resid).astype(f32))
    section_id = lax.axis_index("section")
    all_cands = cand * lax.axis_size("section")
    owner = (
        jnp.arange(all_cands, dtype=jnp.int32)[None, :]
        == (section_id * cand + jnp.arange(cand, dtype=jnp.int32))[:, None]
    ).astype(f32)
    partial_rewards = jnp.sum(attended * gate * readout, axis=(1, 2)) / math.sqrt(total)
    rewards = lax.psum(jnp.sum(owner * partial_rewards[:, None], axis=0), ("seq", "mp", "section"))
    chosen = (pairs[:, :, None] == jnp.arange(all_cands, dtype=jnp.int32)[None, None, :]).astype(
        f32
    )
    paired = jnp.sum(chosen * rewards[None, None, :], axis=-1)
    margin = paired[:, 0] - paired[:, 1]
    target = labels.astype(f32)
    loss = jnp.sum(jax.nn.softplus(margin) - target * margin)
    coeff = jax.nn.sigmoid(margin) - target
    reward_grad = jnp.sum(coeff[:, None] * (chosen[:, 0] - chosen[:, 1]), axis=0)
    own_grad = jnp.sum(owner * reward_grad[None, :], axis=1)
    upstream = (own_grad[:, None, None] * readout * gate).astype(bf16)
    upstream4 = upstream.reshape(cand, frames_dev, heads_here, HD)
    delta = jnp.sum(upstream4.astype(f32) * attended4, axis=-1).transpose(0, 2, 1)

    def backward_block(start, size):
        prob = weights_for(start, size)
        prob_low = prob.astype(bf16)
        dprob = jnp.einsum(
            "cfhe,ckhe->chfk", upstream4, key_slice(values, start, size), preferred_element_type=f32
        )
        dscore = (prob * (dprob - delta[..., None])).astype(bf16)
        dquery = (
            jnp.einsum(
                "chfk,ckhe->cfhe", dscore, key_slice(keys, start, size), preferred_element_type=f32
            )
            * scale
        )
        dkey = jnp.einsum("chfk,cfhe->kche", dscore, query4, preferred_element_type=f32) * scale
        dvalue = jnp.einsum("chfk,cfhe->kche", prob_low, upstream4, preferred_element_type=f32)
        term = jnp.concatenate(
            [dkey.reshape(size, cand, local_width), dvalue.reshape(size, cand, local_width)],
            axis=-1,
        )
        return (dquery, term)

    zero_query = jnp.zeros((cand, frames_dev, heads_here, HD), f32)

    def grad_step(running, index):
        dquery, term = backward_block(index * block, block)
        return (running + dquery, term.astype(bf16))

    grad_query, stored = lax.scan(grad_step, zero_query, jnp.arange(count_blocks))
    stacked = stored.reshape(total, cand, 2 * local_width)
    summed = lax.psum_scatter(
        stacked.astype(f32).astype(jnp.bfloat16), "seq", scatter_dimension=0, tiled=True
    ).astype(jnp.float32)
    grad_key = summed[:, :, :local_width].transpose(1, 0, 2)
    grad_value = summed[:, :, local_width:].transpose(1, 0, 2)
    grads = jnp.stack(
        [grad_query.reshape(cand, frames_dev, local_width), grad_key, grad_value], axis=0
    ).astype(bf16)
    return (grads, rewards, loss.reshape(1))


def solution(mesh):
    placed = (
        P(("groups", "section"), "mp", "seq"),
        P("mp"),
        P("mp", None, None),
        P(None, None, "mp"),
        P("mp"),
        P(("groups", "section")),
        P("groups", None),
        P("groups"),
    )
    return jax.shard_map(
        local,
        mesh=mesh,
        in_specs=placed,
        out_specs=(P(None, ("groups", "section"), "seq", "mp"), P("groups"), P("groups")),
        check_vma=False,
    )
```

profile of v0, /device:TPU:0, one launch (start us, length us, event | category | flops | bytes accessed | tf_op | source)
XLA Modules:
  0.0 278.7 jit_solution(6267920341593110061)
XLA Ops:
  7.2 8.6 %fusion.25 = bf16[1,256,2048]{2,1,0:T(8,128)(2,1)S(1)} fusion(bf16[1,256,2048]{2,1,0:T(8,128)(2,1)} %param.14, f32[256]{0:T(256)} %param.15), kind=kLoop, calls=%fused_computation.40 | loop fusion | flops 3145728 | bytes 2098176 | tf_op jit(solution)/shard_map/convert_element_type | solution.py:46
  17.0 4.9 %collective-permute-start = (bf16[1,256,4]{2,1,0:T(8,128)(2,1)S(1)}, bf16[1,256,4]{2,1,0:T(8,128)(2,1)S(1)}, u32[]{:S(2)}, u32[]{:S(2)}) collective-permute-start(bf16[1,256,4]{2,1,0:T(8,128)(2,1)S(1)} %get-tuple-element.365), channel_id=1, source_target_pairs={{0,4},{4,8},{8,12},{1,5},{5,9},{9,13},{2,6},{6,10},{10,14},{3,7},{... | collective-permute-start | bytes 6152 | tf_op jit(solution)/shard_map/ppermute | solution.py:18
  28.1 3.5 %concatenate.32 = bf16[1,256,2056]{2,1,0:T(8,128)(2,1)} concatenate(bf16[1,256,4]{2,1,0:T(8,128)(2,1)S(1)} %collective-permute-done, bf16[1,256,2048]{2,1,0:T(8,128)(2,1)} %copy-done.5, bf16[1,256,4]{2,1,0:T(8,128)(2,1)S(1)} %collective-permute-done.1), dimensions={2} | concatenate | bytes 2105344 | tf_op jit(solution)/shard_map/concatenate | solution.py:22
  33.9 5.8 %reshape.436 = bf16[1,8,32,257,8]{2,1,4,3,0:T(8,128)(2,1)} reshape(bf16[1,256,2056]{1,2,0:T(8,128)(2,1)} %copy.41) | data formatting | bytes 2105344 | tf_op jit(solution)/shard_map/reshape | solution.py:48
  39.7 6.5 %fusion.53 = (bf16[1,8,256,32,8]{3,1,4,2,0:T(8,128)(2,1)}, bf16[1,8,256,32,8]{3,1,4,2,0:T(8,128)(2,1)}) fusion(bf16[1,8,257,32,8]{3,1,4,2,0:T(8,128)(2,1)} %bitcast.233), kind=kLoop, calls=%fused_computation.102 | loop fusion | bytes 4194304 | tf_op jit(solution)/shard_map/slice | solution.py:51
  46.2 7.7 %copy.42 = bf16[1,8,256,32,8]{2,4,3,1,0:T(8,128)(2,1)} copy(bf16[1,8,256,32,8]{3,1,4,2,0:T(8,128)(2,1)} %get-tuple-element.362) | data formatting | bytes 2097152 | tf_op jit(solution)/shard_map/slice | solution.py:51
  53.9 7.7 %copy.43 = bf16[1,8,256,32,8]{2,4,3,1,0:T(8,128)(2,1)} copy(bf16[1,8,256,32,8]{3,1,4,2,0:T(8,128)(2,1)} %get-tuple-element.363) | data formatting | bytes 2097152 | tf_op jit(solution)/shard_map/slice | solution.py:51
  66.9 3.5 %fusion.31 = bf16[1,256,512]{2,1,0:T(8,128)(2,1)S(1)} fusion(f32[1,256,512]{2,1,0:T(8,128)} %copy.46, f32[512]{0:T(512)S(1)} %fusion.36, f32[256]{0:T(256)S(1)} %add_convert_fusion, pred[512]{0:T(512)(128)(4,1)S(1)} %fusion.33), kind=kLoop, calls=%fused_computation.52 | loop fusion | flops 524288 | bytes 790016 | tf_op jit(solution)/shard_map/convert_element_type | solution.py:64
  71.1 7.3 %all_gather.9 = bf16[1,256,1024]{2,1,0:T(8,128)(2,1)S(1)} all-gather(bf16[1,256,512]{2,1,0:T(8,128)(2,1)S(1)} %fusion.31), channel_id=1, replica_groups=mesh['groups'=2,'seq'=4,'mp'=2,'section'=2] {'mp'}, dimensions={2}, use_global_device_ids=true | all-gather | bytes 786432 | tf_op jit(solution)/shard_map/all_gather | solution.py:65
  82.1 28.3 %all-gather.5.cloned.1.call-done = bf16[1,1024,1,512]{3,1,2,0:T(8,128)(2,1)} async-done(((bf16[1,256,1,512]{3,1,2,0:T(8,128)(2,1)}), bf16[1,1024,1,512]{3,1,2,0:T(8,128)(2,1)}) %all-gather.5.cloned.1.call-update) | async-done | bytes 1048592 | tf_op jit(solution)/shard_map/all_gather | solution.py:71
  112.6 16.1 %while.37 = (s32[]{:T(128)}, f32[1,8,256]{2,1,0:T(8,128)S(1)}, f32[1,8,256]{2,1,0:T(8,128)S(1)}, s32[2]{0:T(128)S(1)}, bf16[1,1024,512]{1,2,0:T(8,128)(2,1)}, /*...) while((s32[]{:T(128)}, f32[1,8,256]{2,1,0:T(8,128)S(1)}, ...), condition=%wide.region_4.5_spmd.clone, body=%wide.region_1.4_spmd.clone.sunk | while | flops 139470848 | bytes 10330286 | solution.py:101
  115.0 2.7 bitcast_reduce_fusion.2
  117.7 3.0 %fusion.86 = f32[8,256]{1,0:T(8,128)S(1)} fusion(f32[8,512,256]{2,1,0:T(8,128)} %get-tuple-element.514, f32[8,256]{1,0:T(8,128)S(1)} %bitcast.239), kind=kLoop, calls=%fused_computation.3.clone.1 | loop fusion | flops 3143680 | bytes 4210688 | tf_op jit(solution)/shard_map/while/body/eval_jaxpr/reduce_sum | solution.py:95
  125.8 2.9 %fusion.86 = f32[8,256]{1,0:T(8,128)S(1)} fusion(f32[8,512,256]{2,1,0:T(8,128)} %get-tuple-element.514, f32[8,256]{1,0:T(8,128)S(1)} %bitcast.239), kind=kLoop, calls=%fused_computation.3.clone.1 | loop fusion | flops 3143680 | bytes 4210688 | tf_op jit(solution)/shard_map/while/body/eval_jaxpr/reduce_sum | solution.py:95
  128.7 10.6 %all-gather.7.cloned.1.call-done = bf16[1,1024,1,512]{3,1,2,0:T(8,128)(2,1)} async-done(((bf16[1,256,1,512]{3,1,2,0:T(8,128)(2,1)}), bf16[1,1024,1,512]{3,1,2,0:T(8,128)(2,1)}) %all-gather.7.cloned.1.call-update) | async-done | bytes 1048592 | tf_op jit(solution)/shard_map/all_gather | solution.py:72
  141.7 13.9 %while.38 = (s32[]{:T(128)}, f32[1,256,8,64]{1,3,2,0:T(8,128)}, s32[2]{0:T(128)S(1)}, bf16[1,1024,512]{1,2,0:T(8,128)(2,1)}, bf16[1,1024,512]{1,2,0:T(8,128)(2,1...) while((s32[]{:T(128)}, f32[1,256,8,64]{1,3,2,0:T(8,128)}, ...), condition=%wide.region_6.7_spmd.clone, body=%wide.region_5.6_spmd.clone.sunk | while | flops 272891904 | bytes 4473021 | solution.py:116
  145.2 3.4 %fusion.90 = f32[1,256,8,64]{1,3,2,0:T(8,128)} fusion(bf16[512,8,64]{0,2,1:T(8,128)(2,1)} %bitcast.236, bf16[512,8,64]{0,2,1:T(8,128)(2,1)} %bitcast.235, f32[8,256]{1,0:T(8,128)S(1)} %bitcast.249, f32[8,256]{1,0:T(8,128)S(1)} %bitcast.245, f32[1,256,8,64]{1,3,2,0:T(8,128)} %get-tuple-element.581, ...), kind=kOutput, calls=%fused_computation.13.clone.1 | convolution fusion | flops 272891904 | bytes 2375681 | tf_op jit(solution)/shard_map/while/body/eval_jaxpr/chfk,ckhe->cfhe/dot_general | solution.py:111
  152.0 3.6 %fusion.90 = f32[1,256,8,64]{1,3,2,0:T(8,128)} fusion(bf16[512,8,64]{0,2,1:T(8,128)(2,1)} %bitcast.236, bf16[512,8,64]{0,2,1:T(8,128)(2,1)} %bitcast.235, f32[8,256]{1,0:T(8,128)S(1)} %bitcast.249, f32[8,256]{1,0:T(8,128)S(1)} %bitcast.245, f32[1,256,8,64]{1,3,2,0:T(8,128)} %get-tuple-element.581, ...), kind=kOutput, calls=%fused_computation.13.clone.1 | convolution fusion | flops 272891904 | bytes 2375681 | tf_op jit(solution)/shard_map/while/body/eval_jaxpr/chfk,ckhe->cfhe/dot_general | solution.py:111
  160.3 31.9 %psum.7 = f32[2]{0:T(128)S(1)} all-reduce(f32[2]{0:T(128)S(1)} %compare_select_fusion.2), channel_id=1, replica_groups=mesh['groups'=2,'seq'=4,'mp'=2,'section'=2] {'seq','mp','section'}, use_global_device_ids=true, to_apply=%region_8.9 | all-reduce | flops 2 | bytes 16 | tf_op jit(solution)/shard_map/psum | solution.py:128
  198.3 25.0 %while.39 = (s32[]{:T(128)}, f32[1,256,8,64]{1,3,2,0:T(8,128)}, bf16[2,512,1,1024]{1,3,2,0:T(8,128)(2,1)}, s32[2]{0:T(128)S(1)}, bf16[1,1024,512]{1,2,0:T(8,128)...) while((s32[]{:T(128)}, f32[1,256,8,64]{1,3,2,0:T(8,128)}, ...), condition=%wide.region_14.15_spmd.clone, body=%wide.region_13.14_spmd.clone.sunk | while | flops 681705472 | bytes 39346984 | solution.py:170
  207.7 3.0 %fusion.101 = f32[1,256,8,64]{1,3,2,0:T(8,128)} fusion(bf16[512,8,64]{0,2,1:T(8,128)(2,1)} %bitcast.227, bf16[8,512,256]{2,1,0:T(8,128)(2,1)} %copy-done.1, f32[1,256,8,64]{1,3,2,0:T(8,128)} %get-tuple-element.620, pred[]{:T(512)S(6)} %compare.19), kind=kOutput, calls=%fused_computation.27.clone.1 | convolution fusion | flops 134610944 | bytes 3670017 | tf_op jit(solution)/shard_map/while/body/eval_jaxpr/chfk,ckhe->cfhe/dot_general | solution.py:151
  220.2 3.1 %fusion.101 = f32[1,256,8,64]{1,3,2,0:T(8,128)} fusion(bf16[512,8,64]{0,2,1:T(8,128)(2,1)} %bitcast.227, bf16[8,512,256]{2,1,0:T(8,128)(2,1)} %copy-done.1, f32[1,256,8,64]{1,3,2,0:T(8,128)} %get-tuple-element.620, pred[]{:T(512)S(6)} %compare.19), kind=kOutput, calls=%fused_computation.27.clone.1 | convolution fusion | flops 134610944 | bytes 3670017 | tf_op jit(solution)/shard_map/while/body/eval_jaxpr/chfk,ckhe->cfhe/dot_general | solution.py:151
  223.3 3.3 %copy.58 = bf16[2,1,128,8,512]{4,3,0,2,1:T(8,128)(2,1)} copy(bf16[2,1,128,8,512]{4,3,2,1,0:T(8,128)(2,1)} %bitcast.70) | data formatting | bytes 4194304 | tf_op jit(solution)/shard_map/reshape | solution.py:171
  227.7 40.2 %reduce-scatter.2.cloned.1.call-done = bf16[256,1,1024]{0,2,1:T(8,128)(2,1)} async-done(((bf16[1024,1,1024]{0,2,1:T(8,128)(2,1)}), bf16[256,1,1024]{0,2,1:T(8,128)(2,1)}) %reduce-scatter.2.cloned.1.call-update) | async-done | bytes 524304 | tf_op jit(solution)/shard_map/reduce_scatter | solution.py:172
  (108 shorter events, 67.8 us)
Async XLA Ops:
  7.2 71.4 %copy-start = (bf16[1024,3,512]{2,0,1:T(8,128)(2,1)S(1)}, bf16[1024,3,512]{2,0,1:T(8,128)(2,1)}, u32[]{:S(2)}) copy-start(bf16[1024,3,512]{2,0,1:T(8,128)(2,1)} %param.17) | copy-start | bytes 9437188
  7.2 103.2 %all-gather.5.cloned.1.call-start = ((), (), s32[]{:S(2)}) async-start(), calls=%async_computation.2 | async-start | bytes 1310720 | tf_op jit(solution)/shard_map/all_gather | solution.py:71
  15.8 1.0 copy-start.5
  17.0 9.6 %collective-permute-start = (bf16[1,256,4]{2,1,0:T(8,128)(2,1)S(1)}, bf16[1,256,4]{2,1,0:T(8,128)(2,1)S(1)}, u32[]{:S(2)}, u32[]{:S(2)}) collective-permute-start(bf16[1,256,4]{2,1,0:T(8,128)(2,1)S(1)} %get-tuple-element.365), channel_id=1, source_target_pairs={{0,4},{4,8},{8,12},{1,5},{5,9},{9,13},{2,6},{6,10},{10,14},{3,7},{... | collective-permute-start | bytes 6152 | tf_op jit(solution)/shard_map/ppermute | solution.py:18
  21.9 6.2 %collective-permute-start.1 = (bf16[1,256,4]{2,1,0:T(8,128)(2,1)S(1)}, bf16[1,256,4]{2,1,0:T(8,128)(2,1)S(1)}, u32[]{:S(2)}, u32[]{:S(2)}) collective-permute-start(bf16[1,256,4]{2,1,0:T(8,128)(2,1)S(1)} %get-tuple-element.364), channel_id=1, source_target_pairs={{4,0},{8,4},{12,8},{5,1},{9,5},{13,9},{6,2},{10,6},{14,10},{7,3},{... | collective-permute-start | bytes 6152 | tf_op jit(solution)/shard_map/ppermute | solution.py:21
  61.7 1.9 copy-start.6
  70.4 0.7 copy-start.7
  78.6 2.1 copy-start.9
  80.6 58.8 %all-gather.7.cloned.1.call-start = ((), (), s32[]{:S(2)}) async-start(), calls=%async_computation.3 | async-start | bytes 1310720 | tf_op jit(solution)/shard_map/all_gather | solution.py:72
  81.8 186.0 %reduce-scatter.2.cloned.1.call-start = ((), (), s32[]{:S(2)}) async-start(), calls=%async_computation.1 | async-start | bytes 2621440 | tf_op jit(solution)/shard_map/reduce_scatter | solution.py:172
  141.7 16.1 %copy-start.8 = (f32[512]{0:T(512)S(1)}, f32[512]{0:T(512)}, u32[]{:S(2)}) copy-start(f32[512]{0:T(512)} %param.18) | copy-start | bytes 6148
  141.7 50.6 %copy-start.10 = (s32[4]{0:T(128)S(1)}, s32[4]{0:T(128)}, u32[]{:S(2)}) copy-start(s32[4]{0:T(128)} %param.21) | copy-start | bytes 52
  155.6 38.7 %copy-start.3 = (bf16[1,256,8,64]{1,3,2,0:T(8,128)(2,1)}, bf16[1,256,8,64]{1,3,2,0:T(8,128)(2,1)S(1)}, u32[]{:S(2)}) copy-start(bf16[1,256,8,64]{1,3,2,0:T(8,128)(2,1)S(1)} %get-tuple-element.656) | copy-start | bytes 786436
  192.2 6.1 %copy-start.11 = (f32[2]{0:T(128)}, f32[2]{0:T(128)S(1)}, u32[]{:S(2)}) copy-start(f32[2]{0:T(128)S(1)} %psum.7) | copy-start | bytes 28
  200.8 2.2 copy-start.2
  203.0 2.1 copy-start.4
  203.8 1.3 copy-start.1
  213.3 2.2 copy-start.2
  215.5 2.1 copy-start.4
  216.3 1.3 copy-start.1
Sparse Core Ops, SparseCore 0:
  80.7 29.6 all-gather.4
  111.9 27.4 all-gather.6
  226.7 41.0 reduce-scatter.1
where the time goes:
time: 280 us; the launch traced here: 279 us
  waiting for transfers between devices  80.7 us (29%)
  local copies, waits for them, and re-layouts  71.9 us (26%)
  blocking collectives  39.2 us (14%)
  other arithmetic  31.1 us (11%)
  matrix products  29.7 us (11%)
  between operations  15.3 us (5%)
  starting transfers between devices  6.74 us (2%)
  loops' own time  4.08 us (1%)
    reduce_scatter x1, waiting for transfers between devices, local(): lax.psum_scatter(stacked.astype(f32).astype(jnp.bfloat16), 'seq', scatter...  40.2 us
    psum x1, blocking collectives, local(): lax.psum(jnp.sum(owner * partial_rewards[:, None], axis=0), ('seq', 'mp',...  31.9 us
    all_gather x1, waiting for transfers between devices, local(): lax.all_gather(qkv[:, :, 1], 'seq', axis=1, tiled=True)  28.3 us
    slice x2, local copies, waits for them, and re-layouts, local(): blocks[:, :, :-1]  14.2 us
    all_gather x1, waiting for transfers between devices, local(): lax.all_gather(qkv[:, :, 2], 'seq', axis=1, tiled=True)  10.6 us
    dot_general x4, matrix products, scores_for(): jnp.einsum('cfhe,ckhe->chfk', query4, key_slice(keys, start, size), prefe...  9.74 us
    dynamic_slice x6, local copies, waits for them, and re-layouts, key_slice(): lax.dynamic_slice_in_dim(source, start, size, 1)  9.22 us
    unnamed x21, local copies, waits for them, and re-layouts  8.64 us
  transfers between devices with their start and end apart: 5, of which 4 were waited for; matrix products, arithmetic and copies ran while one was open for 8% of the time, Pallas kernels for 0%

commit v1 on v0

--- a/solution.py
+++ b/solution.py
@@ -8,6 +8,22 @@
 HD = 64
 EPS = 1e-06
 BASE = 10000.0
+
+
+def ring_gather(x, axis, dim):
+    ways, here, step = (lax.axis_size(axis), lax.axis_index(axis), x.shape[dim])
+    shape = [n * ways if d == dim else n for d, n in enumerate(x.shape)]
+    full = lax.dynamic_update_slice_in_dim(jnp.zeros(shape, x.dtype), x, here * step, axis=dim)
+    going_up = going_down = x
+    for far in range(1, ways // 2 + 1):
+        going_up = lax.ppermute(going_up, axis, [(d, (d + 1) % ways) for d in range(ways)])
+        full = lax.dynamic_update_slice_in_dim(full, going_up, (here - far) % ways * step, axis=dim)
+        if 2 * far < ways:
+            going_down = lax.ppermute(going_down, axis, [(d, (d - 1) % ways) for d in range(ways)])
+            full = lax.dynamic_update_slice_in_dim(
+                full, going_down, (here + far) % ways * step, axis=dim
+            )
+    return full
 
 
 def padded_2(block, sides, width):
@@ -68,7 +84,7 @@
     qkv = (projected * lax.rsqrt(squares + EPS)[:, :, None, None]).astype(bf16)
     query = qkv[:, :, 0]
     keys, values = (
-        lax.all_gather(qkv[:, :, 1], "seq", axis=1, tiled=True),
+        ring_gather(qkv[:, :, 1], "seq", 1),
         lax.all_gather(qkv[:, :, 2], "seq", axis=1, tiled=True),
     )
     total = keys.shape[1]

time: 280 us -> 268 us (0.957)
  waiting for transfers between devices: 80.7 us -> 48.3 us
  local copies, waits for them, and re-layouts: 71.9 us -> 84.7 us
  starting transfers between devices: 6.74 us -> 10.7 us
  blocking collectives: 39.2 us -> 42.5 us
    all_gather x1 -> x0, waiting for transfers between devices: 28.3 us -> none  [local(): lax.all_gather(qkv[:, :, 1], 'seq', axis=1, tiled=True)]
    all_gather x1, waiting for transfers between devices: 10.6 us -> 0.02 us  [local(): lax.all_gather(qkv[:, :, 2], 'seq', axis=1, tiled=True)]
    dynamic_update_slice x0 -> x4, local copies, waits for them, and re-layouts: none -> 6.81 us  [the longest x2 3.38 us: ring_gather(): lax.dynamic_update_slice_in_dim(full, going_up, (here - far) % ways * ste...]
    ppermute x0 -> x3, waiting for transfers between devices: none -> 6.36 us  [the longest x2 6.35 us: ring_gather(): lax.ppermute(going_up, axis, [(d, (d + 1) % ways) for d in range(ways)])]
    ppermute x0 -> x3, local copies, waits for them, and re-layouts: none -> 5.38 us  [the longest x2 3.6 us: ring_gather(): lax.ppermute(going_up, axis, [(d, (d + 1) % ways) for d in range(ways)])]
    ppermute x0 -> x3, starting transfers between devices: none -> 4.18 us  [the longest x1 2.1 us: ring_gather(): lax.ppermute(going_down, axis, [(d, (d - 1) % ways) for d in range(ways)])]
    psum x1, blocking collectives: 31.9 us -> 35.2 us  [local(): lax.psum(jnp.sum(owner * partial_rewards[:, None], axis=0), ('seq', 'mp',...]
    unnamed x21 -> x20, local copies, waits for them, and re-layouts: 8.64 us -> 6.37 us
  transfers between devices with their start and end apart: 5 -> 7, of which waited for: 4 -> 4; matrix products, arithmetic and copies ran while one was open for 8% -> 13% of each run, Pallas kernels for 0% -> 0%
where the time goes in v1:
time: 268 us; the launch traced here: 266 us
  local copies, waits for them, and re-layouts  84.7 us (32%)
  waiting for transfers between devices  48.3 us (18%)
  blocking collectives  42.5 us (16%)
  other arithmetic  31 us (12%)
  matrix products  29.7 us (11%)
  between operations  15.6 us (6%)
  starting transfers between devices  10.7 us (4%)
  loops' own time  4.1 us (2%)
    reduce_scatter x1, waiting for transfers between devices, local(): lax.psum_scatter(stacked.astype(f32).astype(jnp.bfloat16), 'seq', scatter...  40.4 us
    psum x1, blocking collectives, local(): lax.psum(jnp.sum(owner * partial_rewards[:, None], axis=0), ('seq', 'mp',...  35.2 us
    slice x2, local copies, waits for them, and re-layouts, local(): blocks[:, :, :-1]  14.2 us
    dot_general x4, matrix products, scores_for(): jnp.einsum('cfhe,ckhe->chfk', query4, key_slice(keys, start, size), prefe...  9.74 us
    dynamic_slice x6, local copies, waits for them, and re-layouts, key_slice(): lax.dynamic_slice_in_dim(source, start, size, 1)  9.24 us
    convert_element_type x1, other arithmetic, local(): act = (raw + jnp.sin(slope * raw) ** 2 / slope).astype(bf16)  8.61 us
    slice x1, local copies, waits for them, and re-layouts, local(): blocks[:, :, 1:]  7.74 us
    all_gather x1, blocking collectives, local(): whole = lax.all_gather(resid, 'mp', axis=2, tiled=True)  7.28 us
  transfers between devices with their start and end apart: 7, of which 4 were waited for; matrix products, arithmetic and copies ran while one was open for 13% of the time, Pallas kernels for 0%

profile of v1, /device:TPU:0, one launch (start us, length us, event | category | flops | bytes accessed | tf_op | source)
XLA Modules:
  0.0 266.5 jit_solution(2184124154394612736)
XLA Ops:
  7.2 8.6 %fusion.25 = bf16[1,256,2048]{2,1,0:T(8,128)(2,1)S(1)} fusion(bf16[1,256,2048]{2,1,0:T(8,128)(2,1)} %param.14, f32[256]{0:T(256)} %param.15), kind=kLoop, calls=%fused_computation.40 | loop fusion | flops 3145728 | bytes 2098176 | tf_op jit(solution)/shard_map/convert_element_type | solution.py:62
  17.0 4.9 %collective-permute-start = (bf16[1,256,4]{2,1,0:T(8,128)(2,1)S(1)}, bf16[1,256,4]{2,1,0:T(8,128)(2,1)S(1)}, u32[]{:S(2)}, u32[]{:S(2)}) collective-permute-start(bf16[1,256,4]{2,1,0:T(8,128)(2,1)S(1)} %get-tuple-element.353), channel_id=1, source_target_pairs={{0,4},{4,8},{8,12},{1,5},{5,9},{9,13},{2,6},{6,10},{10,14},{3,7},{... | collective-permute-start | bytes 6152 | tf_op jit(solution)/shard_map/ppermute | solution.py:34
  28.1 3.5 %concatenate.32 = bf16[1,256,2056]{2,1,0:T(8,128)(2,1)} concatenate(bf16[1,256,4]{2,1,0:T(8,128)(2,1)S(1)} %collective-permute-done, bf16[1,256,2048]{2,1,0:T(8,128)(2,1)} %copy-done.5, bf16[1,256,4]{2,1,0:T(8,128)(2,1)S(1)} %collective-permute-done.1), dimensions={2} | concatenate | bytes 2105344 | tf_op jit(solution)/shard_map/concatenate | solution.py:38
  33.9 5.8 %reshape.436 = bf16[1,8,32,257,8]{2,1,4,3,0:T(8,128)(2,1)} reshape(bf16[1,256,2056]{1,2,0:T(8,128)(2,1)} %copy.45) | data formatting | bytes 2105344 | tf_op jit(solution)/shard_map/reshape | solution.py:64
  39.7 6.5 %fusion.53 = (bf16[1,8,256,32,8]{3,1,4,2,0:T(8,128)(2,1)}, bf16[1,8,256,32,8]{3,1,4,2,0:T(8,128)(2,1)}) fusion(bf16[1,8,257,32,8]{3,1,4,2,0:T(8,128)(2,1)} %bitcast.234), kind=kLoop, calls=%fused_computation.107 | loop fusion | bytes 4194304 | tf_op jit(solution)/shard_map/slice | solution.py:67
  46.2 7.7 %copy.46 = bf16[1,8,256,32,8]{2,4,3,1,0:T(8,128)(2,1)} copy(bf16[1,8,256,32,8]{3,1,4,2,0:T(8,128)(2,1)} %get-tuple-element.350) | data formatting | bytes 2097152 | tf_op jit(solution)/shard_map/slice | solution.py:67
  53.9 7.7 %copy.47 = bf16[1,8,256,32,8]{2,4,3,1,0:T(8,128)(2,1)} copy(bf16[1,8,256,32,8]{3,1,4,2,0:T(8,128)(2,1)} %get-tuple-element.351) | data formatting | bytes 2097152 | tf_op jit(solution)/shard_map/slice | solution.py:67
  66.9 3.5 %fusion.31 = bf16[1,256,512]{2,1,0:T(8,128)(2,1)S(1)} fusion(f32[1,256,512]{2,1,0:T(8,128)} %copy.50, f32[512]{0:T(512)S(1)} %fusion.36, f32[256]{0:T(256)S(1)} %add_convert_fusion, pred[512]{0:T(512)(128)(4,1)S(1)} %fusion.33), kind=kLoop, calls=%fused_computation.52 | loop fusion | flops 524288 | bytes 790016 | tf_op jit(solution)/shard_map/convert_element_type | solution.py:80
  71.1 7.3 %all_gather.6 = bf16[1,256,1024]{2,1,0:T(8,128)(2,1)S(1)} all-gather(bf16[1,256,512]{2,1,0:T(8,128)(2,1)S(1)} %fusion.31), channel_id=1, replica_groups=mesh['groups'=2,'seq'=4,'mp'=2,'section'=2] {'mp'}, dimensions={2}, use_global_device_ids=true | all-gather | bytes 786432 | tf_op jit(solution)/shard_map/all_gather | solution.py:81
  87.6 4.5 %collective-permute-done.2 = bf16[1,256,512]{2,1,0:T(8,128)(2,1)} collective-permute-done((bf16[1,256,512]{2,1,0:T(8,128)(2,1)}, bf16[1,256,512]{2,1,0:T(8,128)(2,1)}, u32[]{:S(2)}, u32[]{:S(2)}) %collective-permute-start.2) | collective-permute-done | bytes 262176 | tf_op jit(solution)/shard_map/ppermute | solution.py:19
  107.4 15.9 %while.37 = (s32[]{:T(128)}, f32[1,8,256]{2,1,0:T(8,128)S(1)}, f32[1,8,256]{2,1,0:T(8,128)S(1)}, s32[2]{0:T(128)S(1)}, bf16[1,1024,512]{1,2,0:T(8,128)(2,1)}, /*...) while((s32[]{:T(128)}, f32[1,8,256]{2,1,0:T(8,128)S(1)}, ...), condition=%wide.region_4.5_spmd.clone, body=%wide.region_1.4_spmd.clone.sunk | while | flops 139470848 | bytes 10330286 | solution.py:117
  109.7 2.7 %bitcast_reduce_fusion.2 = (f32[8,256]{1,0:T(8,128)S(1)}, f32[8,512,256]{2,1,0:T(8,128)}) fusion(bf16[512,8,64]{0,2,1:T(8,128)(2,1)S(1)} %bitcast.229, bf16[1,256,8,64]{1,3,2,0:T(8,128)(2,1)S(1)} %get-tuple-element.551), kind=kOutput, calls=%fused_computation.1.clone.1 | convolution fusion | flops 136312832 | bytes 4988928 | tf_op jit(solution)/shard_map/while/body/eval_jaxpr/cfhe,ckhe->chfk/dot_general | solution.py:101
  112.4 2.9 %fusion.86 = f32[8,256]{1,0:T(8,128)S(1)} fusion(f32[8,512,256]{2,1,0:T(8,128)} %get-tuple-element.502, f32[8,256]{1,0:T(8,128)S(1)} %bitcast.240), kind=kLoop, calls=%fused_computation.3.clone.1 | loop fusion | flops 3143680 | bytes 4210688 | tf_op jit(solution)/shard_map/while/body/eval_jaxpr/reduce_sum | solution.py:111
  117.7 2.7 %bitcast_reduce_fusion.2 = (f32[8,256]{1,0:T(8,128)S(1)}, f32[8,512,256]{2,1,0:T(8,128)}) fusion(bf16[512,8,64]{0,2,1:T(8,128)(2,1)S(1)} %bitcast.229, bf16[1,256,8,64]{1,3,2,0:T(8,128)(2,1)S(1)} %get-tuple-element.551), kind=kOutput, calls=%fused_computation.1.clone.1 | convolution fusion | flops 136312832 | bytes 4988928 | tf_op jit(solution)/shard_map/while/body/eval_jaxpr/cfhe,ckhe->chfk/dot_general | solution.py:101
  120.4 2.9 %fusion.86 = f32[8,256]{1,0:T(8,128)S(1)} fusion(f32[8,512,256]{2,1,0:T(8,128)} %get-tuple-element.502, f32[8,256]{1,0:T(8,128)S(1)} %bitcast.240), kind=kLoop, calls=%fused_computation.3.clone.1 | loop fusion | flops 3143680 | bytes 4210688 | tf_op jit(solution)/shard_map/while/body/eval_jaxpr/reduce_sum | solution.py:111
  125.6 14.0 %while.38 = (s32[]{:T(128)}, f32[1,256,8,64]{1,3,2,0:T(8,128)}, s32[2]{0:T(128)S(1)}, bf16[1,1024,512]{1,2,0:T(8,128)(2,1)}, bf16[1,1024,512]{1,2,0:T(8,128)(2,1...) while((s32[]{:T(128)}, f32[1,256,8,64]{1,3,2,0:T(8,128)}, ...), condition=%wide.region_6.7_spmd.clone, body=%wide.region_5.6_spmd.clone.sunk | while | flops 272891904 | bytes 4473021 | solution.py:132
  129.1 3.4 %fusion.90 = f32[1,256,8,64]{1,3,2,0:T(8,128)} fusion(bf16[512,8,64]{0,2,1:T(8,128)(2,1)} %bitcast.237, bf16[512,8,64]{0,2,1:T(8,128)(2,1)} %bitcast.236, f32[8,256]{1,0:T(8,128)S(1)} %bitcast.249, f32[8,256]{1,0:T(8,128)S(1)} %bitcast.245, f32[1,256,8,64]{1,3,2,0:T(8,128)} %get-tuple-element.569, ...), kind=kOutput, calls=%fused_computation.13.clone.1 | convolution fusion | flops 272891904 | bytes 2375681 | tf_op jit(solution)/shard_map/while/body/eval_jaxpr/chfk,ckhe->cfhe/dot_general | solution.py:127
  136.0 3.6 %fusion.90 = f32[1,256,8,64]{1,3,2,0:T(8,128)} fusion(bf16[512,8,64]{0,2,1:T(8,128)(2,1)} %bitcast.237, bf16[512,8,64]{0,2,1:T(8,128)(2,1)} %bitcast.236, f32[8,256]{1,0:T(8,128)S(1)} %bitcast.249, f32[8,256]{1,0:T(8,128)S(1)} %bitcast.245, f32[1,256,8,64]{1,3,2,0:T(8,128)} %get-tuple-element.569, ...), kind=kOutput, calls=%fused_computation.13.clone.1 | convolution fusion | flops 272891904 | bytes 2375681 | tf_op jit(solution)/shard_map/while/body/eval_jaxpr/chfk,ckhe->cfhe/dot_general | solution.py:127
  144.2 35.2 %psum.7 = f32[2]{0:T(128)S(1)} all-reduce(f32[2]{0:T(128)S(1)} %compare_select_fusion.2), channel_id=1, replica_groups=mesh['groups'=2,'seq'=4,'mp'=2,'section'=2] {'seq','mp','section'}, use_global_device_ids=true, to_apply=%region_8.9 | all-reduce | flops 2 | bytes 16 | tf_op jit(solution)/shard_map/psum | solution.py:144
  185.6 25.0 %while.39 = (s32[]{:T(128)}, f32[1,256,8,64]{1,3,2,0:T(8,128)}, bf16[2,512,1,1024]{1,3,2,0:T(8,128)(2,1)}, s32[2]{0:T(128)S(1)}, bf16[1,1024,512]{1,2,0:T(8,128)...) while((s32[]{:T(128)}, f32[1,256,8,64]{1,3,2,0:T(8,128)}, ...), condition=%wide.region_14.15_spmd.clone, body=%wide.region_13.14_spmd.clone.sunk | while | flops 681705472 | bytes 39346984 | solution.py:186
  195.0 3.0 %fusion.101 = f32[1,256,8,64]{1,3,2,0:T(8,128)} fusion(bf16[512,8,64]{0,2,1:T(8,128)(2,1)} %bitcast.228, bf16[8,512,256]{2,1,0:T(8,128)(2,1)} %copy-done.1, f32[1,256,8,64]{1,3,2,0:T(8,128)} %get-tuple-element.608, pred[]{:T(512)S(6)} %compare.22), kind=kOutput, calls=%fused_computation.27.clone.1 | convolution fusion | flops 134610944 | bytes 3670017 | tf_op jit(solution)/shard_map/while/body/eval_jaxpr/chfk,ckhe->cfhe/dot_general | solution.py:167
  207.5 3.1 %fusion.101 = f32[1,256,8,64]{1,3,2,0:T(8,128)} fusion(bf16[512,8,64]{0,2,1:T(8,128)(2,1)} %bitcast.228, bf16[8,512,256]{2,1,0:T(8,128)(2,1)} %copy-done.1, f32[1,256,8,64]{1,3,2,0:T(8,128)} %get-tuple-element.608, pred[]{:T(512)S(6)} %compare.22), kind=kOutput, calls=%fused_computation.27.clone.1 | convolution fusion | flops 134610944 | bytes 3670017 | tf_op jit(solution)/shard_map/while/body/eval_jaxpr/chfk,ckhe->cfhe/dot_general | solution.py:167
  210.6 3.3 %copy.63 = bf16[2,1,128,8,512]{4,3,0,2,1:T(8,128)(2,1)} copy(bf16[2,1,128,8,512]{4,3,2,1,0:T(8,128)(2,1)} %bitcast.70) | data formatting | bytes 4194304 | tf_op jit(solution)/shard_map/reshape | solution.py:187
  214.9 40.4 %reduce-scatter.2.cloned.1.call-done = bf16[256,1,1024]{0,2,1:T(8,128)(2,1)} async-done(((bf16[1024,1,1024]{0,2,1:T(8,128)(2,1)}), bf16[256,1,1024]{0,2,1:T(8,128)(2,1)}) %reduce-scatter.2.cloned.1.call-update) | async-done | bytes 524304 | tf_op jit(solution)/shard_map/reduce_scatter | solution.py:188
  (119 shorter events, 83.7 us)
Async XLA Ops:
  7.2 71.4 %copy-start = (bf16[1024,3,512]{2,0,1:T(8,128)(2,1)S(1)}, bf16[1024,3,512]{2,0,1:T(8,128)(2,1)}, u32[]{:S(2)}) copy-start(bf16[1024,3,512]{2,0,1:T(8,128)(2,1)} %param.17) | copy-start | bytes 9437188
  7.2 116.1 %all-gather.3.cloned.1.call-start = ((), (), s32[]{:S(2)}) async-start(), calls=%async_computation.2 | async-start | bytes 1310720 | tf_op jit(solution)/shard_map/all_gather | solution.py:88
  15.8 1.0 copy-start.5
  17.0 9.6 %collective-permute-start = (bf16[1,256,4]{2,1,0:T(8,128)(2,1)S(1)}, bf16[1,256,4]{2,1,0:T(8,128)(2,1)S(1)}, u32[]{:S(2)}, u32[]{:S(2)}) collective-permute-start(bf16[1,256,4]{2,1,0:T(8,128)(2,1)S(1)} %get-tuple-element.353), channel_id=1, source_target_pairs={{0,4},{4,8},{8,12},{1,5},{5,9},{9,13},{2,6},{6,10},{10,14},{3,7},{... | collective-permute-start | bytes 6152 | tf_op jit(solution)/shard_map/ppermute | solution.py:34
  21.9 6.2 %collective-permute-start.1 = (bf16[1,256,4]{2,1,0:T(8,128)(2,1)S(1)}, bf16[1,256,4]{2,1,0:T(8,128)(2,1)S(1)}, u32[]{:S(2)}, u32[]{:S(2)}) collective-permute-start(bf16[1,256,4]{2,1,0:T(8,128)(2,1)S(1)} %get-tuple-element.352), channel_id=1, source_target_pairs={{4,0},{8,4},{12,8},{5,1},{9,5},{13,9},{6,2},{10,6},{14,10},{7,3},{... | collective-permute-start | bytes 6152 | tf_op jit(solution)/shard_map/ppermute | solution.py:37
  61.7 1.9 copy-start.6
  70.4 0.7 copy-start.7
  78.6 6.0 %copy-start.9 = (s32[4,2]{0,1:T(2,128)S(1)}, s32[4,2]{0,1:T(2,128)}, u32[]{:S(2)}) copy-start(s32[4,2]{0,1:T(2,128)} %param.20) | copy-start | bytes 100
  80.5 11.6 %collective-permute-start.2 = (bf16[1,256,512]{2,1,0:T(8,128)(2,1)}, bf16[1,256,512]{2,1,0:T(8,128)(2,1)}, u32[]{:S(2)}, u32[]{:S(2)}) collective-permute-start(bf16[1,256,512]{2,1,0:T(8,128)(2,1)} %get-tuple-element.356), channel_id=1, source_target_pairs={{0,4},{4,8},{8,12},{12,0},{1,5},{5,9},{9,13},{13,1},{2,6},{6,10},{... | collective-permute-start | bytes 786440 | tf_op jit(solution)/shard_map/ppermute | solution.py:19
  82.5 14.3 %collective-permute-start.3 = (bf16[1,256,512]{2,1,0:T(8,128)(2,1)}, bf16[1,256,512]{2,1,0:T(8,128)(2,1)}, u32[]{:S(2)}, u32[]{:S(2)}) collective-permute-start(bf16[1,256,512]{2,1,0:T(8,128)(2,1)} %get-tuple-element.356), channel_id=1, source_target_pairs={{0,12},{4,0},{8,4},{12,8},{1,13},{5,1},{9,5},{13,9},{2,14},{6,2},{... | collective-permute-start | bytes 786440 | tf_op jit(solution)/shard_map/ppermute | solution.py:22
  87.6 167.7 %reduce-scatter.2.cloned.1.call-start = ((), (), s32[]{:S(2)}) async-start(), calls=%async_computation.1 | async-start | bytes 2621440 | tf_op jit(solution)/shard_map/reduce_scatter | solution.py:188
  92.1 11.8 %collective-permute-start.4 = (bf16[1,256,512]{2,1,0:T(8,128)(2,1)}, bf16[1,256,512]{2,1,0:T(8,128)(2,1)}, u32[]{:S(2)}, u32[]{:S(2)}) collective-permute-start(bf16[1,256,512]{2,1,0:T(8,128)(2,1)} %collective-permute-done.2), channel_id=1, source_target_pairs={{0,4},{4,8},{8,12},{12,0},{1,5},{5,9},{9,13},{13,1},{2,6},{6,10},{... | collective-permute-start | bytes 786440 | tf_op jit(solution)/shard_map/ppermute | solution.py:19
  125.6 16.1 %copy-start.8 = (f32[512]{0:T(512)S(1)}, f32[512]{0:T(512)}, u32[]{:S(2)}) copy-start(f32[512]{0:T(512)} %param.18) | copy-start | bytes 6148
  125.6 53.9 %copy-start.10 = (s32[4]{0:T(128)S(1)}, s32[4]{0:T(128)}, u32[]{:S(2)}) copy-start(s32[4]{0:T(128)} %param.21) | copy-start | bytes 52
  139.6 42.0 %copy-start.3 = (bf16[1,256,8,64]{1,3,2,0:T(8,128)(2,1)}, bf16[1,256,8,64]{1,3,2,0:T(8,128)(2,1)S(1)}, u32[]{:S(2)}) copy-start(bf16[1,256,8,64]{1,3,2,0:T(8,128)(2,1)S(1)} %get-tuple-element.641) | copy-start | bytes 786436
  179.5 6.1 %copy-start.11 = (f32[2]{0:T(128)}, f32[2]{0:T(128)S(1)}, u32[]{:S(2)}) copy-start(f32[2]{0:T(128)S(1)} %psum.7) | copy-start | bytes 28
  188.1 2.2 copy-start.2
  190.3 2.1 copy-start.4
  191.1 1.3 copy-start.1
  200.6 2.2 copy-start.2
  202.8 2.1 copy-start.4
  203.6 1.3 copy-start.1
Sparse Core Ops, SparseCore 0:
  87.7 30.3 all-gather.2
  214.0 41.2 reduce-scatter.1
